TPU v7x, 32 devices: a whole 2x2x4 slice. The times are simulated.
32 devices in a mesh: dp: 16 (over z, y, x), seq: 2 (over core).
Axes of the slice: x: 2, y: 2, z: 4, core: 2. Of those that a mesh axis runs over, the one named last changes fastest.
Arguments:
- hidden_in: bfloat16 [16384, 768], P(('dp', 'seq')), may hold values from -6 to 6
- prefix: int32 [16], P('dp'), may hold values from 102 to 512
- w_qkv: bfloat16 [768, 2304], P(('dp', 'seq')), may hold values from -0.21875 to 0.21875
- q_bias: bfloat16 [768], P(('dp', 'seq')), may hold values from -3 to 3
- v_bias: bfloat16 [768], P(('dp', 'seq')), may hold values from -3 to 3
- rel_table: bfloat16 [512, 768], P(('dp', 'seq')), may hold values from -6 to 6
- w_posk: bfloat16 [768, 768], P(('dp', 'seq')), may hold values from -0.21875 to 0.21875
- w_posq: bfloat16 [768, 768], P(('dp', 'seq')), may hold values from -0.21875 to 0.21875
- posq_bias: bfloat16 [768], P(('dp', 'seq')), may hold values from -3 to 3
- w_out: bfloat16 [768, 768], P(('dp', 'seq')), may hold values from -0.875 to 0.875
- out_bias: bfloat16 [768], P(('dp', 'seq')), may hold values from -3 to 3
- norm1_gain: bfloat16 [768], P(('dp', 'seq')), may hold values from 0.5 to 1.5
- norm1_bias: bfloat16 [768], P(('dp', 'seq')), may hold values from -3 to 3
- w_up: bfloat16 [768, 3072], P(('dp', 'seq')), may hold values from -0.21875 to 0.21875
- up_bias: bfloat16 [3072], P(('dp', 'seq')), may hold values from -3 to 3
- w_down: bfloat16 [3072, 768], P(('dp', 'seq')), may hold values from -0.109375 to 0.109375
- down_bias: bfloat16 [768], P(('dp', 'seq')), may hold values from -3 to 3
- norm2_gain: bfloat16 [768], P(('dp', 'seq')), may hold values from 0.5 to 1.5
- norm2_bias: bfloat16 [768], P(('dp', 'seq')), may hold values from -3 to 3
- out_grad: bfloat16 [16384, 768], P(('dp', 'seq')), may hold values from -6 to 6
Outputs:
- hidden_out: bfloat16 [16384, 768], P(('dp', 'seq'))
- in_grad: float32 [16384, 768], P(('dp', 'seq'))
- w_qkv_grad: float32 [768, 2304], P(('dp', 'seq'))
- q_bias_grad: float32 [768], P(('dp', 'seq'))
- v_bias_grad: float32 [768], P(('dp', 'seq'))
- rel_table_grad: float32 [512, 768], P(('dp', 'seq'))
- w_posk_grad: float32 [768, 768], P(('dp', 'seq'))
- w_posq_grad: float32 [768, 768], P(('dp', 'seq'))
- posq_bias_grad: float32 [768], P(('dp', 'seq'))
- w_out_grad: float32 [768, 768], P(('dp', 'seq'))
- out_bias_grad: float32 [768], P(('dp', 'seq'))
- norm1_gain_grad: float32 [768], P(('dp', 'seq'))
- norm1_bias_grad: float32 [768], P(('dp', 'seq'))
- w_up_grad: float32 [768, 3072], P(('dp', 'seq'))
- up_bias_grad: float32 [3072], P(('dp', 'seq'))
- w_down_grad: float32 [3072, 768], P(('dp', 'seq'))
- down_bias_grad: float32 [768], P(('dp', 'seq'))
- norm2_gain_grad: float32 [768], P(('dp', 'seq'))
- norm2_bias_grad: float32 [768], P(('dp', 'seq'))
All inputs are finite; a program needn't handle non-finite values.
Results may differ from a plain program's by a relative error of at most 0.023.
Values may be sent and summed in bfloat16 or wider, within the bound.
No kernel may reach another device: no remote copies, remote signals or barrier semaphores. Data moves between devices by JAX's collectives and lax.ppermute only.
A program may use at most 192 MiB of HBM per device.

v0:
```python
import math

import jax
import jax.numpy as jnp
from jax import lax
from jax.sharding import PartitionSpec as P

D = 768
HEADS = 12
HEAD_DIM = 64
SPAN = 256


eps_norm = 1e-07


def normalize(value, gain, shift):
    average = jnp.mean(value, axis=-1, keepdims=True)
    centred = value - average
    variance = jnp.mean(centred * centred, axis=-1, keepdims=True)
    return centred * lax.rsqrt(variance + eps_norm) * gain + shift


def gelu_exact(value):
    return jax.nn.gelu(value, approximate=False)


def product(left, right):
    return jnp.dot(left, right, preferred_element_type=jnp.float32)


def inner_first(left, right):
    return lax.dot_general(
        left, right, (((0,), (0,)), ((), ())), preferred_element_type=jnp.float32
    )


def inner_last(left, right):
    return lax.dot_general(
        left, right, (((1,), (1,)), ((), ())), preferred_element_type=jnp.float32
    )


def split_heads(matrix):
    return matrix.reshape(matrix.shape[0], HEADS, HEAD_DIM).transpose(1, 0, 2)


def join_heads(stacked):
    return stacked.transpose(1, 0, 2).reshape(stacked.shape[1], D)


def column_sums(matrix):
    return jnp.sum(matrix.astype(jnp.float32), axis=0)


def shards(
    hidden_in,
    prefix,
    w_qkv,
    q_bias,
    v_bias,
    rel_table,
    w_posk,
    w_posq,
    posq_bias,
    w_out,
    out_bias,
    norm1_gain,
    norm1_bias,
    w_up,
    up_bias,
    w_down,
    down_bias,
    norm2_gain,
    norm2_bias,
    out_grad,
):
    gathered = (
        lax.all_gather(w_qkv, ("dp", "seq"), axis=0, tiled=True),
        lax.all_gather(q_bias, ("dp", "seq"), axis=0, tiled=True),
        lax.all_gather(v_bias, ("dp", "seq"), axis=0, tiled=True),
        lax.all_gather(rel_table, ("dp", "seq"), axis=0, tiled=True),
        lax.all_gather(w_posk, ("dp", "seq"), axis=0, tiled=True),
        lax.all_gather(w_posq, ("dp", "seq"), axis=0, tiled=True),
        lax.all_gather(posq_bias, ("dp", "seq"), axis=0, tiled=True),
        lax.all_gather(w_out, ("dp", "seq"), axis=0, tiled=True),
        lax.all_gather(out_bias, ("dp", "seq"), axis=0, tiled=True),
        lax.all_gather(norm1_gain, ("dp", "seq"), axis=0, tiled=True),
        lax.all_gather(norm1_bias, ("dp", "seq"), axis=0, tiled=True),
        lax.all_gather(w_up, ("dp", "seq"), axis=0, tiled=True),
        lax.all_gather(up_bias, ("dp", "seq"), axis=0, tiled=True),
        lax.all_gather(w_down, ("dp", "seq"), axis=0, tiled=True),
        lax.all_gather(down_bias, ("dp", "seq"), axis=0, tiled=True),
        lax.all_gather(norm2_gain, ("dp", "seq"), axis=0, tiled=True),
        lax.all_gather(norm2_bias, ("dp", "seq"), axis=0, tiled=True),
    )
    (
        full_qkv,
        full_qb,
        full_vb,
        full_table,
        full_posk,
        full_posq,
        full_pqb,
        full_out,
        full_ob,
        full_g1,
        full_b1,
        full_up,
        full_ub,
        full_down,
        full_db,
        full_g2,
        full_b2,
    ) = gathered
    row_count = hidden_in.shape[0]
    groups = lax.axis_size("seq")
    seq_length = row_count * groups
    seq_rank = lax.axis_index("seq")
    prefix_len = prefix[0]
    score_scale = 1.0 / math.sqrt(3 * HEAD_DIM)
    buckets = 2 * SPAN
    window = row_count + buckets
    first_row = seq_rank * row_count
    query_pos = first_row + jnp.arange(row_count, dtype=jnp.int32)
    key_pos = jnp.arange(seq_length, dtype=jnp.int32)
    visible = (key_pos[None, :] < prefix_len) | (key_pos[None, :] <= query_pos[:, None])
    padded_cols = jnp.arange(seq_length + buckets, dtype=jnp.int32)
    below_window = padded_cols[None, :] < first_row

    def skew_table(table, row_total, offset, col_total):
        shifted = jnp.pad(
            jnp.flip(table, axis=1), ((0, 0), (row_count, row_count - 1)), mode="edge"
        )
        stride = shifted.shape[1] - 1
        flattened = shifted.reshape(-1)
        picked = lax.slice_in_dim(flattened, offset, offset + row_total * stride)
        return picked.reshape(row_total, stride)[:, :col_total]

    def pos_terms(table_a, table_w, edge_terms):
        band_terms = (
            skew_table(table_a, row_count, row_count - 1, window)
            + skew_table(table_w, window, window - 1, row_count).T
        )
        low_side = table_a[:, buckets - 1 : buckets] + jnp.pad(edge_terms[0], (SPAN, SPAN))[None, :]
        high_side = table_a[:, 0:1] + jnp.pad(edge_terms[1], (SPAN, SPAN))[None, :]
        backdrop = jnp.where(below_window, low_side, high_side)
        placed = lax.dynamic_update_slice(
            backdrop, band_terms, (jnp.zeros((), jnp.int32), first_row)
        )
        return placed[:, SPAN : SPAN + seq_length]

    pos_keys = product(full_table, full_posk).astype(jnp.bfloat16)
    pos_queries = (product(full_table, full_posq) + full_pqb.astype(jnp.float32)).astype(
        jnp.bfloat16
    )
    merged = product(hidden_in, full_qkv)
    queries = (merged[:, :D] + full_qb.astype(jnp.float32)).astype(jnp.bfloat16)
    keys_local = merged[:, D : 2 * D].astype(jnp.bfloat16)
    values_local = (merged[:, 2 * D :] + full_vb.astype(jnp.float32)).astype(jnp.bfloat16)
    keys_all, values_all = (
        lax.all_gather(keys_local, "seq", axis=0, tiled=True),
        lax.all_gather(values_local, "seq", axis=0, tiled=True),
    )
    query_heads = split_heads(queries)
    key_heads = split_heads(keys_all)
    value_heads = split_heads(values_all)
    posk_heads = split_heads(pos_keys)
    posq_heads = split_heads(pos_queries)

    def head_scores(query_h, key_h, posk_h, posq_h):
        content = inner_last(query_h, key_h)
        table_a = inner_last(query_h, posk_h)
        key_padded = jnp.pad(key_h, ((SPAN, SPAN), (0, 0)))
        key_window = lax.dynamic_slice_in_dim(key_padded, first_row, window, 0)
        table_w = inner_last(key_window, posq_h)
        end_rows = jnp.stack([posq_h[0], posq_h[buckets - 1]])
        edge_terms = inner_last(end_rows, key_h)
        raw = content + pos_terms(table_a, table_w, edge_terms)
        masked = jnp.where(visible, raw * score_scale, -jnp.inf)
        return (masked, table_a, table_w, edge_terms, key_window, end_rows)

    def head_forward(operands):
        query_h, key_h, value_h, posk_h, posq_h = operands
        scores = head_scores(query_h, key_h, posk_h, posq_h)[0]
        highest = jnp.max(scores, axis=1, keepdims=True)
        expo = jnp.exp(scores - highest)
        totals = jnp.sum(expo, axis=1, keepdims=True)
        probs_low = (expo / totals).astype(jnp.bfloat16)
        return (product(probs_low, value_h), (highest + jnp.log(totals))[:, 0])

    contexts, log_totals = lax.map(
        head_forward, (query_heads, key_heads, value_heads, posk_heads, posq_heads)
    )
    context = join_heads(contexts).astype(jnp.bfloat16)
    hidden_f = hidden_in.astype(jnp.float32)
    residual1 = hidden_f + product(context, full_out) + full_ob.astype(jnp.float32)
    gain1 = full_g1.astype(jnp.float32)
    shift1 = full_b1.astype(jnp.float32)
    normed = normalize(residual1, gain1, shift1)
    normed_low = normed.astype(jnp.bfloat16)
    expanded = product(normed_low, full_up) + full_ub.astype(jnp.float32)
    activated = gelu_exact(expanded).astype(jnp.bfloat16)
    residual2 = normed + product(activated, full_down) + full_db.astype(jnp.float32)
    gain2 = full_g2.astype(jnp.float32)
    shift2 = full_b2.astype(jnp.float32)
    hidden_out = normalize(residual2, gain2, shift2).astype(jnp.bfloat16)
    regathered = (
        lax.all_gather(w_qkv, ("dp", "seq"), axis=0, tiled=True),
        lax.all_gather(q_bias, ("dp", "seq"), axis=0, tiled=True),
        lax.all_gather(v_bias, ("dp", "seq"), axis=0, tiled=True),
        lax.all_gather(rel_table, ("dp", "seq"), axis=0, tiled=True),
        lax.all_gather(w_posk, ("dp", "seq"), axis=0, tiled=True),
        lax.all_gather(w_posq, ("dp", "seq"), axis=0, tiled=True),
        lax.all_gather(posq_bias, ("dp", "seq"), axis=0, tiled=True),
        lax.all_gather(w_out, ("dp", "seq"), axis=0, tiled=True),
        lax.all_gather(out_bias, ("dp", "seq"), axis=0, tiled=True),
        lax.all_gather(norm1_gain, ("dp", "seq"), axis=0, tiled=True),
        lax.all_gather(norm1_bias, ("dp", "seq"), axis=0, tiled=True),
        lax.all_gather(w_up, ("dp", "seq"), axis=0, tiled=True),
        lax.all_gather(up_bias, ("dp", "seq"), axis=0, tiled=True),
        lax.all_gather(w_down, ("dp", "seq"), axis=0, tiled=True),
        lax.all_gather(down_bias, ("dp", "seq"), axis=0, tiled=True),
        lax.all_gather(norm2_gain, ("dp", "seq"), axis=0, tiled=True),
        lax.all_gather(norm2_bias, ("dp", "seq"), axis=0, tiled=True),
    )
    (
        back_qkv,
        back_qb,
        back_vb,
        back_table,
        back_posk,
        back_posq,
        back_pqb,
        back_out,
        back_ob,
        back_g1,
        back_b1,
        back_up,
        back_ub,
        back_down,
        back_db,
        back_g2,
        back_b2,
    ) = regathered
    _, pull_second = jax.vjp(normalize, residual2, gain2, shift2)
    d_res2, d_gain2, d_shift2 = pull_second(out_grad.astype(jnp.float32))
    d_reduced = d_res2.astype(jnp.bfloat16)
    d_wdown = inner_first(activated, d_reduced)
    d_down_bias = column_sums(d_reduced)
    d_activated = inner_last(d_reduced, back_down)
    _, pull_gelu = jax.vjp(gelu_exact, expanded)
    d_expanded = pull_gelu(d_activated)[0].astype(jnp.bfloat16)
    d_wup = inner_first(normed_low, d_expanded)
    d_up_bias = column_sums(d_expanded)
    d_normed = inner_last(d_expanded, back_up) + d_res2
    _, pull_first = jax.vjp(normalize, residual1, gain1, shift1)
    d_res1, d_gain1, d_shift1 = pull_first(d_normed)
    d_attended = d_res1.astype(jnp.bfloat16)
    d_wout = inner_first(context, d_attended)
    d_out_bias = column_sums(d_attended)
    d_context = inner_last(d_attended, back_out).astype(jnp.bfloat16)
    dctx_heads = split_heads(d_context)

    def head_backward(operands):
        query_h, key_h, value_h, posk_h, posq_h, log_total, dctx_h = operands
        scores, table_a, table_w, edge_terms, key_window, end_rows = head_scores(
            query_h, key_h, posk_h, posq_h
        )
        probs = jnp.exp(scores - log_total[:, None])
        probs_low = probs.astype(jnp.bfloat16)
        d_probs = inner_last(dctx_h, value_h)
        d_value = inner_first(probs_low, dctx_h)
        row_dot = jnp.sum(probs * d_probs, axis=1, keepdims=True)
        d_raw = (probs * (d_probs - row_dot) * score_scale).astype(jnp.bfloat16)
        _, pull_terms = jax.vjp(pos_terms, table_a, table_w, edge_terms)
        d_table_a, d_table_w, d_edges = pull_terms(d_raw.astype(jnp.float32))
        d_table_a = d_table_a.astype(jnp.bfloat16)
        d_table_w = d_table_w.astype(jnp.bfloat16)
        d_edges = d_edges.astype(jnp.bfloat16)
        d_query = product(d_raw, key_h) + product(d_table_a, posk_h)
        window_grad = product(d_table_w, posq_h)
        key_canvas = jnp.zeros((seq_length + buckets, HEAD_DIM), jnp.float32)
        placed_grad = lax.dynamic_update_slice(
            key_canvas, window_grad, (first_row, jnp.zeros((), jnp.int32))
        )
        d_key = (
            inner_first(d_raw, query_h)
            + placed_grad[SPAN : SPAN + seq_length]
            + inner_first(d_edges, end_rows)
        )
        d_posk = inner_first(d_table_a, query_h)
        end_grads = product(d_edges, key_h)
        d_posq = inner_first(d_table_w, key_window)
        d_posq = d_posq.at[0].add(end_grads[0]).at[buckets - 1].add(end_grads[1])
        return (d_query, d_key, d_value, d_posk, d_posq)

    d_q_heads, d_k_heads, d_v_heads, d_posk_heads, d_posq_heads = lax.map(
        head_backward,
        (query_heads, key_heads, value_heads, posk_heads, posq_heads, log_totals, dctx_heads),
    )
    d_queries = join_heads(d_q_heads).astype(jnp.bfloat16)
    d_keys_part, d_values_part = (
        lax.psum_scatter(
            join_heads(d_k_heads).astype(jnp.bfloat16), "seq", scatter_dimension=0, tiled=True
        ).astype(jnp.float32),
        lax.psum_scatter(
            join_heads(d_v_heads).astype(jnp.bfloat16), "seq", scatter_dimension=0, tiled=True
        ).astype(jnp.float32),
    )
    d_keys = d_keys_part.astype(jnp.bfloat16)
    d_values = d_values_part.astype(jnp.bfloat16)
    d_merged = jnp.concatenate([d_queries, d_keys, d_values], axis=1)
    d_wqkv = inner_first(hidden_in, d_merged)
    d_q_bias = column_sums(d_queries)
    d_v_bias = column_sums(d_values)
    in_grad = d_res1 + inner_last(d_merged, back_qkv)
    d_posk_rows, d_posq_rows = (
        lax.psum_scatter(join_heads(d_posk_heads), ("dp", "seq"), scatter_dimension=0, tiled=True),
        lax.psum_scatter(join_heads(d_posq_heads), ("dp", "seq"), scatter_dimension=0, tiled=True),
    )
    d_posk_low = d_posk_rows.astype(jnp.bfloat16)
    d_posq_low = d_posq_rows.astype(jnp.bfloat16)
    rel_table_grad = inner_last(d_posk_low, back_posk) + inner_last(d_posq_low, back_posq)
    d_wposk = inner_first(rel_table, d_posk_low)
    d_wposq = inner_first(rel_table, d_posq_low)
    d_posq_bias = column_sums(d_posq_low)
    summed = (
        lax.psum_scatter(d_wqkv, ("dp", "seq"), scatter_dimension=0, tiled=True),
        lax.psum_scatter(d_q_bias, ("dp", "seq"), scatter_dimension=0, tiled=True),
        lax.psum_scatter(d_v_bias, ("dp", "seq"), scatter_dimension=0, tiled=True),
        lax.psum_scatter(d_wposk, ("dp", "seq"), scatter_dimension=0, tiled=True),
        lax.psum_scatter(d_wposq, ("dp", "seq"), scatter_dimension=0, tiled=True),
        lax.psum_scatter(d_posq_bias, ("dp", "seq"), scatter_dimension=0, tiled=True),
        lax.psum_scatter(d_wout, ("dp", "seq"), scatter_dimension=0, tiled=True),
        lax.psum_scatter(d_out_bias, ("dp", "seq"), scatter_dimension=0, tiled=True),
        lax.psum_scatter(d_gain1, ("dp", "seq"), scatter_dimension=0, tiled=True),
        lax.psum_scatter(d_shift1, ("dp", "seq"), scatter_dimension=0, tiled=True),
        lax.psum_scatter(d_wup, ("dp", "seq"), scatter_dimension=0, tiled=True),
        lax.psum_scatter(d_up_bias, ("dp", "seq"), scatter_dimension=0, tiled=True),
        lax.psum_scatter(d_wdown, ("dp", "seq"), scatter_dimension=0, tiled=True),
        lax.psum_scatter(d_down_bias, ("dp", "seq"), scatter_dimension=0, tiled=True),
        lax.psum_scatter(d_gain2, ("dp", "seq"), scatter_dimension=0, tiled=True),
        lax.psum_scatter(d_shift2, ("dp", "seq"), scatter_dimension=0, tiled=True),
    )
    return (
        hidden_out,
        in_grad,
        summed[0],
        summed[1],
        summed[2],
        rel_table_grad,
        summed[3],
        summed[4],
        summed[5],
        summed[6],
        summed[7],
        summed[8],
        summed[9],
        summed[10],
        summed[11],
        summed[12],
        summed[13],
        summed[14],
        summed[15],
    )


def solution(mesh):
    placed = (
        P(("dp", "seq"), None),
        P("dp"),
        P(("dp", "seq"), None),
        P(("dp", "seq")),
        P(("dp", "seq")),
        P(("dp", "seq"), None),
        P(("dp", "seq"), None),
        P(("dp", "seq"), None),
        P(("dp", "seq")),
        P(("dp", "seq"), None),
        P(("dp", "seq")),
        P(("dp", "seq")),
        P(("dp", "seq")),
        P(("dp", "seq"), None),
        P(("dp", "seq")),
        P(("dp", "seq"), None),
        P(("dp", "seq")),
        P(("dp", "seq")),
        P(("dp", "seq")),
        P(("dp", "seq"), None),
    )
    return jax.shard_map(
        shards,
        mesh=mesh,
        in_specs=placed,
        out_specs=(
            P(("dp", "seq"), None),
            P(("dp", "seq"), None),
            P(("dp", "seq"), None),
            P(("dp", "seq")),
            P(("dp", "seq")),
            P(("dp", "seq"), None),
            P(("dp", "seq"), None),
            P(("dp", "seq"), None),
            P(("dp", "seq")),
            P(("dp", "seq"), None),
            P(("dp", "seq")),
            P(("dp", "seq")),
            P(("dp", "seq")),
            P(("dp", "seq"), None),
            P(("dp", "seq")),
            P(("dp", "seq"), None),
            P(("dp", "seq")),
            P(("dp", "seq")),
            P(("dp", "seq")),
        ),
        check_vma=False,
    )
```

profile of v0, /device:TPU:0, one launch (start us, length us, event | category | flops | bytes accessed | tf_op | source)
XLA Modules:
  0.0 4852.3 jit_solution(16146835806083036027)
XLA Ops:
  17.9 42.5 all-reduce.44
  85.2 42.2 all_gather.66
  139.0 47.0 all-gather.13.cloned.1.call-done
  213.7 1124.1 %while.41 = (s32[]{:T(128)}, bf16[12,512,64]{1,2,0:T(8,128)(2,1)}, f32[12,512]{1,0:T(8,128)}, bf16[12,512,64]{2,1,0:T(8,128)(2,1)}, bf16[12,1024,64]{2,1,0:T(8,1...) while((s32[]{:T(128)}, bf16[12,512,64]{1,2,0:T(8,128)(2,1)}, ...), condition=%wide.region_3.4_spmd.clone.clone, body=%wide.region_0.3_spmd.clone.sunk.clone | while | flops 248510976 | bytes 140022704 | solution.py:192
  1341.0 19.8 multiply_convert_fusion.1
  1389.9 2504.3 %while.42 = (s32[]{:T(128)}, bf16[12,512,64]{1,2,0:T(8,128)(2,1)}, bf16[12,1024,64]{1,2,0:T(8,128)(2,1)}, bf16[12,1024,64]{1,2,0:T(8,128)(2,1)}, f32[12,512,64]{...) while((s32[]{:T(128)}, bf16[12,512,64]{1,2,0:T(8,128)(2,1)}, ...), condition=%wide.region_22.23_spmd.clone.clone, body=%wide.region_12.22_spmd.clone.sunk.clone | while | flops 665221760 | bytes 286488128 | solution.py:298
  1527.5 15.5 rev.67
  1735.7 15.5 rev.67
  1943.7 15.5 rev.67
  2151.7 15.5 rev.67
  2567.7 15.5 rev.67
  2775.7 15.5 rev.67
  2983.8 15.5 rev.67
  3191.7 15.5 rev.67
  3607.9 15.5 rev.67
  3902.6 93.7 %reduce-scatter.33.cloned.1.call-done = f32[16,768]{1,0:T(8,128)} async-done(((f32[512,768]{1,0:T(8,128)}), f32[16,768]{1,0:T(8,128)}) %reduce-scatter.33.cloned.1.call-update) | async-done | bytes 49168
  3999.8 99.1 %reduce-scatter.35.cloned.1.call-done = f32[16,768]{1,0:T(8,128)} async-done(((f32[512,768]{1,0:T(8,128)}), f32[16,768]{1,0:T(8,128)}) %reduce-scatter.35.cloned.1.call-update) | async-done | bytes 49168
  4142.2 41.6 all-reduce.43
  4195.1 33.6 reduce-scatter.25.cloned.1.call-done
  4228.7 104.4 %reduce-scatter.37.cloned.1.call-done = f32[24,768]{1,0:T(8,128)} async-done(((f32[768,768]{1,0:T(8,128)}), f32[24,768]{1,0:T(8,128)}) %reduce-scatter.37.cloned.1.call-update) | async-done | bytes 73744
  4333.1 104.5 %reduce-scatter.39.cloned.1.call-done = f32[24,768]{1,0:T(8,128)} async-done(((f32[768,768]{1,0:T(8,128)}), f32[24,768]{1,0:T(8,128)}) %reduce-scatter.39.cloned.1.call-update) | async-done | bytes 73744
  4437.6 141.5 %reduce-scatter.27.cloned.1.call-done = f32[24,3072]{1,0:T(8,128)} async-done(((f32[768,3072]{1,0:T(8,128)}), f32[24,3072]{1,0:T(8,128)}) %reduce-scatter.27.cloned.1.call-update) | async-done | bytes 294928 | tf_op jit(solution)/shard_map/reduce_scatter | solution.py:339
  4579.1 141.5 %reduce-scatter.29.cloned.1.call-done = f32[96,768]{1,0:T(8,128)} async-done(((f32[3072,768]{1,0:T(8,128)}), f32[96,768]{1,0:T(8,128)}) %reduce-scatter.29.cloned.1.call-update) | async-done | bytes 294928 | tf_op jit(solution)/shard_map/reduce_scatter | solution.py:341
  4720.6 124.7 %reduce-scatter.31.cloned.1.call-done = f32[24,2304]{1,0:T(8,128)} async-done(((f32[768,2304]{1,0:T(8,128)}), f32[24,2304]{1,0:T(8,128)}) %reduce-scatter.31.cloned.1.call-update) | async-done | bytes 221200
  (1880 shorter events, 3633.9 us)
Async XLA Ops:
  7.2 66.6 %all-gather.9.cloned.1.call-start = ((), (), s32[]{:S(2)}) async-start(), calls=%async_computation.10 | async-start | bytes 3649536 | tf_op jit(solution)/shard_map/all_gather | solution.py:79
  7.9 125.2 %all-gather.15.cloned.1.call-start = ((), (), s32[]{:S(2)}) async-start(), calls=%async_computation.13 | async-start | bytes 1216512 | tf_op jit(solution)/shard_map/all_gather | solution.py:84
  8.7 177.4 %all-gather.13.cloned.1.call-start = ((), (), s32[]{:S(2)}) async-start(), calls=%async_computation.12 | async-start | bytes 1216512 | tf_op jit(solution)/shard_map/all_gather | solution.py:83
  9.4 187.3 %all-gather.17.cloned.1.call-start = ((), (), s32[]{:S(2)}) async-start(), calls=%async_computation.14 | async-start | bytes 2359296 | tf_op jit(solution)/shard_map/all_gather | solution.py:163
  80.4 128.8 %all-gather.11.cloned.1.call-start = ((), (), s32[]{:S(2)}) async-start(), calls=%async_computation.11 | async-start | bytes 2359296 | tf_op jit(solution)/shard_map/all_gather | solution.py:162
  82.9 1255.0 %all-gather.19.cloned.1.call-start = ((), (), s32[]{:S(2)}) async-start(), calls=%async_computation.15 | async-start | bytes 1216512 | tf_op jit(solution)/shard_map/all_gather | solution.py:86
  83.4 1257.5 %all-gather.21.cloned.1.call-start = ((), (), s32[]{:S(2)}) async-start(), calls=%async_computation.16 | async-start | bytes 4866048 | tf_op jit(solution)/shard_map/all_gather | solution.py:90
  84.2 1276.6 %all-gather.23.cloned.1.call-start = ((), (), s32[]{:S(2)}) async-start(), calls=%async_computation.17 | async-start | bytes 4866048 | tf_op jit(solution)/shard_map/all_gather | solution.py:92
  84.9 3911.4 %reduce-scatter.33.cloned.1.call-start = ((), (), s32[]{:S(2)}) async-start(), calls=%async_computation.24 | async-start | bytes 1622016
  85.1 103.9 %copy-start.3 = (bf16[12,512,64]{1,2,0:T(8,128)(2,1)}, bf16[12,512,64]{1,2,0:T(8,128)(2,1)S(1)}, u32[]{:S(2)}) copy-start(bf16[12,512,64]{1,2,0:T(8,128)(2,1)S(1)} %fusion.136) | copy-start | bytes 2359300
  213.7 1124.2 %copy-start.52 = (f32[768]{0:T(1024)S(1)}, f32[768]{0:T(1024)}, u32[]{:S(2)}) copy-start(f32[768]{0:T(1024)} %convert_element_type.211) | copy-start | bytes 9220
  1340.6 43.8 copy-start.5
  3897.3 201.6 %reduce-scatter.35.cloned.1.call-start = ((), (), s32[]{:S(2)}) async-start(), calls=%async_computation.25 | async-start | bytes 1622016
  3899.0 221.5 %reduce-scatter.23.cloned.1.call-start = ((), (), s32[]{:S(2)}) async-start(), calls=%async_computation.19 | async-start | bytes 2359296 | tf_op jit(solution)/shard_map/reduce_scatter | solution.py:307
  3899.7 221.8 %reduce-scatter.21.cloned.1.call-start = ((), (), s32[]{:S(2)}) async-start(), calls=%async_computation.18 | async-start | bytes 2359296 | tf_op jit(solution)/shard_map/reduce_scatter | solution.py:304
  3900.3 328.4 %reduce-scatter.25.cloned.1.call-start = ((), (), s32[]{:S(2)}) async-start(), calls=%async_computation.20 | async-start | bytes 2433024 | tf_op jit(solution)/shard_map/reduce_scatter | solution.py:335
  3902.6 94.8 %copy-start.22 = (bf16[16,768]{1,0:T(8,128)(2,1)S(1)}, bf16[16,768]{1,0:T(8,128)(2,1)}, u32[]{:S(2)}) copy-start(bf16[16,768]{1,0:T(8,128)(2,1)} %param.33) | copy-start | bytes 73732
  3902.6 430.5 %reduce-scatter.37.cloned.1.call-start = ((), (), s32[]{:S(2)}) async-start(), calls=%async_computation.26 | async-start | bytes 2433024
  3999.8 437.8 %reduce-scatter.39.cloned.1.call-start = ((), (), s32[]{:S(2)}) async-start(), calls=%async_computation.27 | async-start | bytes 2433024
  4102.4 476.7 %reduce-scatter.27.cloned.1.call-start = ((), (), s32[]{:S(2)}) async-start(), calls=%async_computation.21 | async-start | bytes 9732096 | tf_op jit(solution)/shard_map/reduce_scatter | solution.py:339
  4111.0 609.6 %reduce-scatter.29.cloned.1.call-start = ((), (), s32[]{:S(2)}) async-start(), calls=%async_computation.22 | async-start | bytes 9732096 | tf_op jit(solution)/shard_map/reduce_scatter | solution.py:341
  4120.5 724.8 %reduce-scatter.31.cloned.1.call-start = ((), (), s32[]{:S(2)}) async-start(), calls=%async_computation.23 | async-start | bytes 7299072
  4136.4 53.2 %copy-start.8 = (f32[512,768]{1,0:T(8,128)S(1)}, f32[512,768]{1,0:T(8,128)}, u32[]{:S(2)}) copy-start(f32[512,768]{1,0:T(8,128)} %copy-done.7) | copy-start | bytes 4718596
  4139.6 50.1 %copy-start.46 = (f32[512]{0:T(512)S(1)}, f32[512]{0:T(512)}, u32[]{:S(2)}) copy-start(f32[512]{0:T(512)} %copy-done.45) | copy-start | bytes 6148
  (209 other events, 676.7 us)
Sparse Core Ops, SparseCore 0:
  10.9 62.7 all-gather.8
  76.6 53.6 all-gather.14
  133.2 52.7 all-gather.12
  188.0 8.6 all-gather.16
  198.1 10.9 all-gather.10
  211.9 55.0 all-gather.18
  269.9 62.5 all-gather.20
  335.4 61.9 all-gather.22
  3897.4 98.9 reduce-scatter.32
  4002.0 96.8 reduce-scatter.34
  4101.2 7.9 reduce-scatter.22
  4111.3 10.1 reduce-scatter.20
  4127.4 101.2 reduce-scatter.24
  4234.4 98.6 reduce-scatter.36
  4338.8 98.7 reduce-scatter.38
  4443.9 135.1 reduce-scatter.26
  4585.4 135.1 reduce-scatter.28
  4726.7 118.5 reduce-scatter.30
where the time goes:
time: 4910 us; the launch traced here: 4850 us
  local copies, waits for them, and re-layouts  2770 us (56%)
  waiting for transfers between devices  921 us (19%)
  other arithmetic  582 us (12%)
  matrix products  413 us (8%)
  blocking collectives  126 us (3%)
    rev x72, local copies, waits for them, and re-layouts, skew_table(): jnp.flip(table, axis=1)  670 us
    unnamed x23, waiting for transfers between devices  532 us
    reshape x72, local copies, waits for them, and re-layouts, skew_table(): flattened = shifted.reshape(-1)  509 us
    reshape x72, local copies, waits for them, and re-layouts, skew_table(): return picked.reshape(row_total, stride)[:, :col_total]  448 us
    concatenate x48, local copies, waits for them, and re-layouts, skew_table(): jnp.pad(jnp.flip(table, axis=1), ((0, 0), (row_count, row_count - 1)), mo...  217 us
    concatenate x48, other arithmetic, skew_table(): jnp.pad(jnp.flip(table, axis=1), ((0, 0), (row_count, row_count - 1)), mo...  211 us
    slice x48, local copies, waits for them, and re-layouts, skew_table(): picked = lax.slice_in_dim(flattened, offset, offset + row_total * stride)  190 us
    dot_general x114, matrix products, inner_last(): lax.dot_general(left, right, (((1,), (1,)), ((), ())), preferred_element_...  172 us
  transfers between devices with their start and end apart: 18, of which 13 were waited for; matrix products, arithmetic and copies ran while one was open for 25% of the time, Pallas kernels for 0%

commit v1 on v0

--- a/solution.py
+++ b/solution.py
@@ -3,12 +3,18 @@
 import jax
 import jax.numpy as jnp
 from jax import lax
+from jax.experimental import pallas as pl
+from jax.experimental.pallas import tpu as pltpu
 from jax.sharding import PartitionSpec as P
 
 D = 768
 HEADS = 12
 HEAD_DIM = 64
 SPAN = 256
+TILE = 128
+BLOCK = 256
+BAND = 768
+PAIR = 2 * HEAD_DIM
 
 
 eps_norm = 1e-07
@@ -53,7 +59,582 @@
     return jnp.sum(matrix.astype(jnp.float32), axis=0)
 
 
-def shards(
+def nn(left, right):
+    return lax.dot_general(
+        left, right, (((1,), (0,)), ((), ())), preferred_element_type=jnp.float32
+    )
+
+
+def nt(left, right):
+    return lax.dot_general(
+        left, right, (((1,), (1,)), ((), ())), preferred_element_type=jnp.float32
+    )
+
+
+def unit_matrix(size, reverse=False):
+    rows = lax.broadcasted_iota(jnp.int32, (size, size), 0)
+    cols = lax.broadcasted_iota(jnp.int32, (size, size), 1)
+    if reverse:
+        cols = size - 1 - cols
+    return jnp.where(rows == cols, 1.0, 0.0).astype(jnp.bfloat16)
+
+
+def head_lanes(head):
+    lanes = lax.broadcasted_iota(jnp.int32, (1, PAIR), 1)
+    return lanes // HEAD_DIM == head
+
+
+def head_rows(head):
+    rows = lax.broadcasted_iota(jnp.int32, (HEAD_DIM, PAIR), 0)
+    cols = lax.broadcasted_iota(jnp.int32, (HEAD_DIM, PAIR), 1)
+    return jnp.where(cols == rows + head * HEAD_DIM, 1.0, 0.0).astype(jnp.bfloat16)
+
+
+def key_tiles(block, length):
+    return max(length // 2, (block + 1) * BLOCK) // TILE
+
+
+def tile_seen(query_tile, key_tile, length):
+    return key_tile < key_tiles(query_tile * TILE // BLOCK, length)
+
+
+def skewed(window):
+    return pltpu.roll(window, 0, 1, stride=1, stride_axis=0)
+
+
+def forward_body(prefix_ref, q_ref, k_ref, v_ref, pk_ref, pq_ref, ctx_ref, p_ref, wb_ref, far_ref, s_ref):
+    length = q_ref.shape[0]
+    head = pl.program_id(1)
+    mine = head_lanes(head)
+    prefix = prefix_ref[0]
+    eye = unit_matrix(TILE)
+    eye_block = unit_matrix(BLOCK)
+    zero = jnp.zeros((), jnp.bfloat16)
+    scale = math.log2(math.e) / math.sqrt(3 * HEAD_DIM)
+    for tile in range(length // TILE):
+        rows = slice(tile * TILE, (tile + 1) * TILE)
+        table = nt(jnp.where(mine, k_ref[rows, :], zero), pq_ref[...])
+        wb_ref[rows, :] = skewed(table)
+        wb_ref[rows, 0:TILE] = table[:, BAND - TILE :]
+        far_ref[rows, :] = table[:, 0:TILE]
+    v_cols = nt(jnp.where(lax.broadcasted_iota(jnp.int32, (PAIR, PAIR), 0) // HEAD_DIM == head, unit_matrix(PAIR), zero), v_ref[...]).astype(jnp.bfloat16)
+    for block in range(length // BLOCK):
+        cols = slice(block * BLOCK, (block + 1) * BLOCK)
+        q_own = jnp.where(mine, q_ref[cols, :], zero)
+        skews, highs, lows = [], [], []
+        for sub in range(2):
+            table = nt(q_own[sub * TILE : (sub + 1) * TILE], pk_ref[...])
+            skews.append(skewed(table).astype(jnp.bfloat16))
+            highs.append(table[:, 0:TILE].astype(jnp.bfloat16))
+            lows.append(table[:, BAND - TILE :].astype(jnp.bfloat16))
+        count = key_tiles(block, length)
+        highest = None
+        for tile in range(count):
+            rows = slice(tile * TILE, (tile + 1) * TILE)
+            parts_a, parts_b = [], []
+            for sub in range(2):
+                step = 2 * block + sub - tile
+                if step >= 3:
+                    parts_a.append(highs[sub])
+                    parts_b.append(wb_ref[rows, 0:TILE])
+                elif step <= -3:
+                    parts_a.append(lows[sub])
+                    parts_b.append(far_ref[rows, :])
+                else:
+                    at = 384 - TILE * step
+                    parts_a.append(skews[sub][:, at : at + TILE])
+                    at = 384 + TILE * step
+                    parts_b.append(wb_ref[rows, at : at + TILE])
+            right = jnp.concatenate([jnp.concatenate(parts_a, axis=0), q_own], axis=1)
+            left = jnp.concatenate([eye, k_ref[rows, :]], axis=1)
+            raw = nt(left, right) + jnp.concatenate(parts_b, axis=1)
+            if (tile + 1) * TILE > block * BLOCK + 1:
+                keys = tile * TILE + lax.broadcasted_iota(jnp.int32, (TILE, BLOCK), 0)
+                queries = block * BLOCK + lax.broadcasted_iota(jnp.int32, (TILE, BLOCK), 1)
+                raw = jnp.where((keys < prefix) | (keys <= queries), raw, -jnp.inf)
+            s_ref[rows, :] = raw
+            top = jnp.max(raw, axis=0, keepdims=True)
+            highest = top if highest is None else jnp.maximum(highest, top)
+        total = jnp.zeros((1, BLOCK), jnp.float32)
+        for tile in range(count):
+            rows = slice(tile * TILE, (tile + 1) * TILE)
+            expo = jnp.exp2((s_ref[rows, :] - highest) * scale)
+            s_ref[rows, :] = expo
+            total = total + jnp.sum(expo, axis=0, keepdims=True)
+        inverse = 1.0 / total
+        for tile in range(count):
+            rows = slice(tile * TILE, (tile + 1) * TILE)
+            p_ref[rows, cols] = (s_ref[rows, :] * inverse).astype(jnp.bfloat16)
+        seen = count * TILE
+        ctx_cols = nn(v_cols[:, :seen], p_ref[0:seen, cols]).astype(jnp.bfloat16)
+        ctx = nt(eye_block, ctx_cols).astype(jnp.bfloat16)
+
+        @pl.when(head == 0)
+        def _():
+            ctx_ref[cols, :] = ctx
+
+        @pl.when(head == 1)
+        def _():
+            ctx_ref[cols, :] = ctx_ref[cols, :] + ctx
+
+
+def attention_forward(prefix, q, k, v, pk, pq):
+    length, width = q.shape
+    pairs = width // PAIR
+    tall = pl.BlockSpec((length, PAIR), lambda p, h: (0, p))
+    band = pl.BlockSpec((BAND, PAIR), lambda p, h: (0, p))
+    return pl.pallas_call(
+        forward_body,
+        grid=(pairs, 2),
+        in_specs=[pl.BlockSpec(memory_space=pltpu.SMEM), tall, tall, tall, band, band],
+        out_specs=[tall, pl.BlockSpec((None, length, length), lambda p, h: (2 * p + h, 0, 0))],
+        out_shape=[
+            jax.ShapeDtypeStruct((length, width), jnp.bfloat16),
+            jax.ShapeDtypeStruct((2 * pairs, length, length), jnp.bfloat16),
+        ],
+        scratch_shapes=[
+            pltpu.VMEM((length, BAND), jnp.float32),
+            pltpu.VMEM((length, TILE), jnp.float32),
+            pltpu.VMEM((length, BLOCK), jnp.float32),
+        ],
+        compiler_params=pltpu.CompilerParams(dimension_semantics=("arbitrary", "arbitrary"), vmem_limit_bytes=48 << 20),
+        name="attention_forward",
+    )(prefix, q, k, v, pk, pq)
+
+
+def backward_body(q_ref, k_ref, v_ref, dctx_ref, p_ref, pk_ref, pq_ref, dq_ref, dk_ref, dv_ref, dpk_ref, dpq_ref, dr_ref, dk_acc, dv_acc):
+    length = q_ref.shape[0]
+    head = pl.program_id(1)
+    mine = head_lanes(head)
+    flip = unit_matrix(TILE, reverse=True)
+    pick = head_rows(head)
+    bf = jnp.bfloat16
+    zero = jnp.zeros((), bf)
+    scale = 1.0 / math.sqrt(3 * HEAD_DIM)
+    back = BAND - (TILE - 1)
+    blank = jnp.zeros((TILE, TILE), bf)
+    dk_acc[...] = jnp.zeros_like(dk_acc)
+    dv_acc[...] = jnp.zeros_like(dv_acc)
+    dpk_ref[...] = jnp.zeros_like(dpk_ref)
+    dpq_ref[...] = jnp.zeros_like(dpq_ref)
+
+    def put(ref, rows, value):
+        @pl.when(head == 0)
+        def _():
+            ref[rows, :] = jnp.where(mine, value, 0.0).astype(bf)
+
+        @pl.when(head == 1)
+        def _():
+            ref[rows, :] = jnp.where(mine, value.astype(bf), ref[rows, :])
+
+    for block in range(length // BLOCK):
+        cols = slice(block * BLOCK, (block + 1) * BLOCK)
+        count = key_tiles(block, length)
+        seen = count * TILE
+        dctx = dctx_ref[cols, :]
+        v_own = jnp.where(mine, v_ref[0:seen, :], zero)
+        probs_low = p_ref[0:seen, cols]
+        probs = probs_low.astype(jnp.float32)
+        d_probs = nt(v_own, dctx)
+        row_dot = jnp.sum(probs * d_probs, axis=0, keepdims=True)
+        d_raw = (probs * ((d_probs - row_dot) * scale)).astype(bf)
+        dr_ref[0:seen, cols] = d_raw
+        dv_acc[0:seen, :] += nn(probs_low, dctx)
+        dk_acc[0:seen, :] += nn(d_raw, q_ref[cols, :])
+        for sub in range(2):
+            tile = 2 * block + sub
+            own = slice(tile * TILE, (tile + 1) * TILE)
+            turned_f = nt(flip, dr_ref[0:seen, own])
+            turned = turned_f.astype(bf)
+            dq = nn(turned, k_ref[0:seen, :])
+
+            def piece(key_tile):
+                return turned[:, key_tile * TILE : (key_tile + 1) * TILE]
+
+            band = [blank]
+            for step in (2, 1, 0, -1, -2):
+                key_tile = tile - step
+                band.append(piece(key_tile) if 0 <= key_tile < count else blank)
+            spread = pltpu.roll(jnp.concatenate(band, axis=1), back, 1, stride=1, stride_axis=0)
+            near = [turned_f[:, t * TILE : (t + 1) * TILE] for t in range(count) if tile - t >= 3]
+            far = [turned_f[:, t * TILE : (t + 1) * TILE] for t in range(count) if tile - t <= -3]
+            spread = add_edges(spread, near, far)
+            dq = dq + nn(spread, pk_ref[...])
+            put(dq_ref, own, nn(flip, dq.astype(bf)))
+            q_turned = nn(flip, q_ref[own, :]).astype(bf)
+            q_cols = nt(pick, q_turned).astype(bf)
+            dpk_ref[...] += nn(q_cols, spread)
+    tiles = length // TILE
+    for key_tile in range(tiles):
+        rows = slice(key_tile * TILE, (key_tile + 1) * TILE)
+
+        def held(query_tile):
+            return dr_ref[rows, query_tile * TILE : (query_tile + 1) * TILE]
+
+        seen_by = [t for t in range(tiles) if tile_seen(t, key_tile, length)]
+        band = [blank]
+        for step in (-2, -1, 0, 1, 2):
+            query_tile = key_tile + step
+            band.append(held(query_tile) if query_tile in seen_by else blank)
+        later = [held(t).astype(jnp.float32) for t in seen_by if t - key_tile >= 3]
+        earlier = [held(t).astype(jnp.float32) for t in seen_by if t - key_tile <= -3]
+        spread = pltpu.roll(nn(flip, jnp.concatenate(band, axis=1)).astype(bf), back, 1, stride=1, stride_axis=0)
+        flat = lambda parts: [nn(flip, sum(parts[1:], parts[0]).astype(bf))] if parts else []
+        spread = add_edges(spread, flat(earlier), flat(later))
+        d_key = nn(flip, nn(spread, pq_ref[...]).astype(bf))
+        put(dk_ref, rows, dk_acc[rows, :] + d_key)
+        k_turned = nn(flip, k_ref[rows, :]).astype(bf)
+        k_cols = nt(pick, k_turned).astype(bf)
+        dpq_ref[...] += nn(k_cols, spread)
+        put(dv_ref, rows, dv_acc[rows, :])
+
+
+def add_edges(spread, first, last):
+    parts = [spread[:, 0:TILE], spread[:, TILE : BAND - TILE], spread[:, BAND - TILE :]]
+    for place, tiles in ((0, first), (2, last)):
+        if tiles:
+            total = parts[place].astype(jnp.float32)
+            for tile in tiles:
+                total = total + tile
+            parts[place] = total.astype(jnp.bfloat16)
+    return jnp.concatenate(parts, axis=1)
+
+
+def attention_backward(q, k, v, dctx, probs, pk, pq):
+    length, width = q.shape
+    pairs = width // PAIR
+    tall = pl.BlockSpec((length, PAIR), lambda p, h: (0, p))
+    band = pl.BlockSpec((BAND, PAIR), lambda p, h: (0, p))
+    table = pl.BlockSpec((HEAD_DIM, BAND), lambda p, h: (2 * p + h, 0))
+    flat = jax.ShapeDtypeStruct((length, width), jnp.bfloat16)
+    wide = jax.ShapeDtypeStruct((width, BAND), jnp.float32)
+    return pl.pallas_call(
+        backward_body,
+        grid=(pairs, 2),
+        in_specs=[tall, tall, tall, tall, pl.BlockSpec((None, length, length), lambda p, h: (2 * p + h, 0, 0)), band, band],
+        out_specs=[tall, tall, tall, table, table],
+        out_shape=[flat, flat, flat, wide, wide],
+        scratch_shapes=[
+            pltpu.VMEM((length, length), jnp.bfloat16),
+            pltpu.VMEM((length, PAIR), jnp.float32),
+            pltpu.VMEM((length, PAIR), jnp.float32),
+        ],
+        compiler_params=pltpu.CompilerParams(dimension_semantics=("arbitrary", "arbitrary"), vmem_limit_bytes=48 << 20),
+        name="attention_backward",
+    )(q, k, v, dctx, probs, pk, pq)
+
+
+CORES = [(0, 1), (1, 0)]
+
+
+def swap(value):
+    return lax.ppermute(value, "seq", CORES)
+
+
+def ordered(core, own, other, axis=0):
+    return jnp.concatenate(
+        [jnp.where(core == 0, own, other), jnp.where(core == 0, other, own)], axis=axis
+    )
+
+
+def half_of(core, matrix, axis):
+    size = matrix.shape[axis] // 2
+    return lax.dynamic_slice_in_dim(matrix, core * size, size, axis)
+
+
+def gather_pair(value, bit, mask):
+    other = lax.ppermute(value, "dp", [(i, i ^ mask) for i in range(16)])
+    return jnp.stack([jnp.where(bit == 0, value, other), jnp.where(bit == 0, other, value)])
+
+
+def gather_line(value, place):
+    below, above = [value], [value]
+    for step in range(1, 4):
+        up = [(i, i + 4) for i in range(12) if i // 4 >= step - 1]
+        down = [(i + 4, i) for i in range(12) if i // 4 <= 3 - step]
+        below.append(lax.ppermute(below[-1], "dp", up))
+        above.append(lax.ppermute(above[-1], "dp", down))
+    blocks = []
+    for block in range(4):
+        options = [below[z - block] if z >= block else above[block - z] for z in range(4)]
+        blocks.append(lax.select_n(place, *options))
+    return jnp.stack(blocks)
+
+
+def scatter_pair(value, bit, mask):
+    keep = jnp.where(bit == 0, value[0], value[1])
+    give = jnp.where(bit == 0, value[1], value[0])
+    other = lax.ppermute(give, "dp", [(i, i ^ mask) for i in range(16)])
+    return (keep.astype(jnp.float32) + other.astype(jnp.float32)).astype(value.dtype)
+
+
+def scatter_line(value, place):
+    def block(offset):
+        options = [value[min(max(z + offset, 0), 3)] for z in range(4)]
+        return lax.select_n(place, *options).astype(jnp.float32)
+
+    up = down = None
+    for step in range(3, 0, -1):
+        to_above, to_below = block(step), block(-step)
+        if up is not None:
+            to_above = to_above + up.astype(jnp.float32)
+            to_below = to_below + down.astype(jnp.float32)
+        ups = [(i, i + 4) for i in range(12) if i // 4 + step <= 3]
+        downs = [(i + 4, i) for i in range(12) if i // 4 + 1 - step >= 0]
+        up = lax.ppermute(to_above.astype(value.dtype), "dp", ups)
+        down = lax.ppermute(to_below.astype(value.dtype), "dp", downs)
+    return block(0) + up.astype(jnp.float32) + down.astype(jnp.float32)
+
+
+def gather_chips(value, first):
+    chip = lax.axis_index("dp")
+    z, y, x = chip // 4, (chip // 2) % 2, chip % 2
+    line = gather_line(value, z)
+    if first == "x":
+        grid = gather_pair(gather_pair(line, x, 1), y, 2)
+        grid = jnp.moveaxis(grid, (0, 1, 2), (1, 2, 0))
+    else:
+        grid = gather_pair(gather_pair(line, y, 2), x, 1)
+        grid = jnp.moveaxis(grid, (0, 1, 2), (2, 1, 0))
+    return grid.reshape((16,) + value.shape)
+
+
+def scatter_chips(value, first):
+    chip = lax.axis_index("dp")
+    z, y, x = chip // 4, (chip // 2) % 2, chip % 2
+    grid = value.reshape((4, 2, 2) + value.shape[1:])
+    if first == "x":
+        grid = jnp.moveaxis(grid, (0, 1, 2), (2, 1, 0))
+        line = scatter_pair(scatter_pair(grid, x, 1), y, 2)
+    else:
+        grid = jnp.moveaxis(grid, (0, 1, 2), (2, 0, 1))
+        line = scatter_pair(scatter_pair(grid, y, 2), x, 1)
+    return scatter_line(line, z)
+
+
+def norm_parts(value):
+    average = jnp.mean(value, axis=-1, keepdims=True)
+    centred = value - average
+    variance = jnp.mean(centred * centred, axis=-1, keepdims=True)
+    inverse = lax.rsqrt(variance + eps_norm)
+    return centred * inverse, inverse
+
+
+def norm_back(unit, inverse, gain, grad):
+    scaled = grad * gain
+    mean_grad = jnp.mean(scaled, axis=-1, keepdims=True)
+    mean_along = jnp.mean(scaled * unit, axis=-1, keepdims=True)
+    return inverse * (scaled - mean_grad - unit * mean_along)
+
+
+def head_split(
+    hidden_in, prefix, w_qkv, q_bias, v_bias, rel_table, w_posk, w_posq, posq_bias, w_out, out_bias,
+    norm1_gain, norm1_bias, w_up, up_bias, w_down, down_bias, norm2_gain, norm2_bias, out_grad,
+):
+    bf = jnp.bfloat16
+    f32 = jnp.float32
+    core = lax.axis_index("seq")
+    rows = w_qkv.shape[0]
+    units = w_down.shape[0]
+    table_rows = rel_table.shape[0]
+    chips = 16
+    half = D // 2
+    ff_half = chips * units
+    buckets = 2 * SPAN
+
+    small = jnp.concatenate(
+        [q_bias, v_bias, posq_bias, out_bias, norm1_gain, norm1_bias, down_bias, norm2_gain, norm2_bias, up_bias]
+    )
+    small = jnp.pad(small, (0, half - small.shape[0]))[None, :]
+    last_rows = rows - table_rows - 1
+
+    def columns(side):
+        qkv = w_qkv.reshape(rows, 3, 2, half)[:, :, side].reshape(rows, 3 * half)
+        corner = jnp.concatenate(
+            [rel_table[:, side * half : (side + 1) * half], small, jnp.zeros((last_rows, half), bf)], axis=0
+        )
+        cut = slice(side * half, (side + 1) * half)
+        up = w_up.reshape(rows, chips, 2, units)[:, :, side].reshape(rows, ff_half)
+        return (
+            jnp.concatenate([qkv, w_posk[:, cut], w_posq[:, cut], corner], axis=1),
+            jnp.concatenate([w_out[:, cut], up], axis=1),
+        )
+
+    early0, late0 = columns(0)
+    early1, late1 = columns(1)
+    early_own = jnp.where(core == 0, early0, early1)
+    early_got = swap(jnp.where(core == 0, early1, early0))
+    late_own = jnp.where(core == 0, late0, late1)
+    late_got = swap(jnp.where(core == 0, late1, late0))
+
+    def both_cores(own, got):
+        first = gather_chips(jnp.where(core == 0, own, got), "x")
+        second = gather_chips(jnp.where(core == 0, got, own), "y")
+        return jnp.stack([first, second], axis=1).reshape(chips * 2 * rows, own.shape[1])
+
+    hidden_all = ordered(core, hidden_in, swap(hidden_in))
+    early = both_cores(early_own, early_got)
+    w_qkv_own = early[:, : 3 * half]
+    w_pos_own = early[:, 3 * half : 5 * half]
+    corner = early[:, 5 * half :].reshape(2 * chips, rows, half)
+    table_half = corner[:, :table_rows].reshape(buckets, half)
+    table = ordered(core, table_half, swap(table_half), axis=1)
+    vectors = corner[:, table_rows].astype(f32)
+    lists = vectors[:, : 9 * rows].reshape(2 * chips, 9, rows).transpose(1, 0, 2).reshape(9, D)
+    qb, vb, pqb, ob, gain1, shift1, db, gain2, shift2 = [lists[i] for i in range(9)]
+    up_lists = vectors[:, 9 * rows : 9 * rows + units].reshape(chips, 2, units)
+    ub = jnp.where(core == 0, up_lists[:, 0], up_lists[:, 1]).reshape(ff_half)
+
+    late = both_cores(late_own, late_got)
+    down_left = gather_chips(w_down[:, :half], "x").reshape(ff_half, half)
+    down_right = gather_chips(w_down[:, half:], "y").reshape(ff_half, half)
+    w_down_own = jnp.concatenate([down_left, down_right], axis=1)
+    out_columns = late[:, :half]
+    w_out_own = ordered(
+        core, half_of(core, out_columns, 0), swap(half_of(1 - core, out_columns, 0)), axis=1
+    )
+    w_up_own = late[:, half:]
+
+    band = lax.broadcasted_iota(jnp.int32, (BAND, buckets), 0)
+    bucket = lax.broadcasted_iota(jnp.int32, (BAND, buckets), 1)
+    chosen = (jnp.clip(SPAN + 384 - band, 0, buckets - 1) == bucket).astype(bf)
+    pos_shift = jnp.concatenate([jnp.zeros((half,), f32), half_of(core, pqb, 0)])
+    pos = (product(table, w_pos_own) + pos_shift).astype(bf)
+    pos_band = product(chosen, pos).astype(bf)
+    pk, pq = pos_band[:, :half], pos_band[:, half:]
+
+    qkv_shift = jnp.concatenate([half_of(core, qb, 0), jnp.zeros((half,), f32), half_of(core, vb, 0)])
+    merged = (product(hidden_all, w_qkv_own) + qkv_shift).astype(bf)
+    q, k, v = merged[:, :half], merged[:, half : 2 * half], merged[:, 2 * half :]
+    context, probs = attention_forward(prefix, q, k, v, pk, pq)
+
+    def summed_rows(left, multiply):
+        given = swap(multiply(half_of(1 - core, left, 0)))
+        return multiply(half_of(core, left, 0)) + given
+
+    hidden_f = hidden_in.astype(f32)
+    residual1 = hidden_f + summed_rows(context, lambda part: product(part, w_out_own)) + ob
+    unit1, inverse1 = norm_parts(residual1)
+    normed = unit1 * gain1 + shift1
+    normed_low = normed.astype(bf)
+    normed_all = ordered(core, normed_low, swap(normed_low))
+    expanded = product(normed_all, w_up_own) + ub
+    normal_cdf = 0.5 * lax.erfc(-expanded * math.sqrt(0.5))
+    activated = (expanded * normal_cdf).astype(bf)
+    slope = (
+        normal_cdf + expanded * jnp.exp(-0.5 * expanded * expanded) * (1.0 / math.sqrt(2.0 * math.pi))
+    ).astype(bf)
+    residual2 = normed + summed_rows(activated, lambda part: product(part, w_down_own)) + db
+    unit2, inverse2 = norm_parts(residual2)
+    hidden_out = (unit2 * gain2 + shift2).astype(bf)
+
+    grad = out_grad.astype(f32)
+    d_res2 = norm_back(unit2, inverse2, gain2, grad)
+    d_gain2 = jnp.sum(grad * unit2, axis=0)
+    d_shift2 = jnp.sum(grad, axis=0)
+    d_reduced = d_res2.astype(bf)
+    d_down_bias = column_sums(d_reduced)
+    reduced_all = ordered(core, d_reduced, swap(d_reduced))
+    d_expanded = (inner_last(reduced_all, w_down_own) * slope.astype(f32)).astype(bf)
+    d_normed = summed_rows(d_expanded, lambda part: inner_last(part, w_up_own)) + d_res2
+    d_wdown = inner_first(activated, reduced_all).astype(bf)
+    d_wup = inner_first(normed_all, d_expanded).astype(bf)
+    d_up_bias = column_sums(d_expanded)
+    d_res1 = norm_back(unit1, inverse1, gain1, d_normed)
+    d_gain1 = jnp.sum(d_normed * unit1, axis=0)
+    d_shift1 = jnp.sum(d_normed, axis=0)
+    d_attended = d_res1.astype(bf)
+    d_out_bias = column_sums(d_attended)
+    attended_all = ordered(core, d_attended, swap(d_attended))
+    d_context = inner_last(attended_all, w_out_own).astype(bf)
+    d_wout_rows = inner_first(context, attended_all).astype(bf)
+    d_wout = ordered(
+        core, half_of(core, d_wout_rows, 1), swap(half_of(1 - core, d_wout_rows, 1)), axis=0
+    )
+
+    def spread_cores(matrix):
+        split = matrix.reshape(chips, 2, rows, matrix.shape[1])
+        return scatter_chips(split[:, 0], "x"), scatter_chips(split[:, 1], "y")
+
+    def rejoin(first, second):
+        own = jnp.where(core == 0, first, second)
+        got = swap(jnp.where(core == 0, second, first))
+        return jnp.where(core == 0, own, got), jnp.where(core == 0, got, own)
+
+    late_grads = spread_cores(jnp.concatenate([d_wout, d_wup], axis=1))
+    down_parts = d_wdown.reshape(chips, units, D)
+    g_wdown = jnp.concatenate(
+        [scatter_chips(down_parts[:, :, :half], "x"), scatter_chips(down_parts[:, :, half:], "y")], axis=1
+    )
+
+    d_q, d_k, d_v, d_pk, d_pq = attention_backward(q, k, v, d_context, probs, pk, pq)
+    d_merged = jnp.concatenate([d_q, d_k, d_v], axis=1)
+    in_grad = d_res1 + summed_rows(d_merged, lambda part: inner_last(part, w_qkv_own))
+    d_wqkv = inner_first(hidden_all, d_merged).astype(bf)
+    d_q_bias = column_sums(d_q)
+    d_v_bias = column_sums(d_v)
+    d_band = jnp.concatenate([d_pk, d_pq], axis=0).astype(bf)
+    d_pos = lax.dot_general(
+        chosen, d_band, (((0,), (1,)), ((), ())), preferred_element_type=f32
+    )
+    d_posq_bias = jnp.sum(d_pos[:, half:], axis=0)
+    d_pos_low = d_pos.astype(bf)
+    d_wpos = inner_first(table, d_pos_low).astype(bf)
+    d_table_all = inner_last(d_pos_low, w_pos_own).astype(bf)
+    d_table = (
+        half_of(core, d_table_all, 1).astype(f32)
+        + swap(half_of(1 - core, d_table_all, 1)).astype(f32)
+    ).astype(bf)
+
+    def whole(part):
+        blank = jnp.zeros_like(part)
+        return ordered(core, part, blank)
+
+    lists_grad = jnp.stack(
+        [
+            whole(d_q_bias), whole(d_v_bias), whole(d_posq_bias), d_out_bias, d_gain1, d_shift1,
+            d_down_bias, d_gain2, d_shift2,
+        ]
+    ).reshape(9, chips, 2, rows).transpose(2, 1, 0, 3).reshape(2, chips, 9 * rows)
+    vector_own = jnp.where(core == 0, lists_grad[0], lists_grad[1])
+    vector_got = swap(jnp.where(core == 0, lists_grad[1], lists_grad[0]))
+    vector = jnp.concatenate(
+        [vector_own + vector_got, d_up_bias.reshape(chips, units), jnp.zeros((chips, half - 9 * rows - units), f32)],
+        axis=1,
+    ).astype(bf)
+    vector = jnp.broadcast_to(vector[:, None, None, :], (chips, 2, 1, half))
+    corner_grad = jnp.concatenate(
+        [d_table.reshape(chips, 2, table_rows, half), vector, jnp.zeros((chips, 2, last_rows, half), bf)], axis=2
+    ).reshape(chips * 2 * rows, half)
+    early_grads = spread_cores(jnp.concatenate([d_wqkv, d_wpos, corner_grad], axis=1))
+    vector_sum = jnp.where(core == 0, early_grads[0], early_grads[1])[table_rows, 5 * half :]
+    early_left, early_right = rejoin(*early_grads)
+    late_left, late_right = rejoin(*late_grads)
+
+    def side_by_side(left, right, at, count):
+        pieces = []
+        for index in range(count):
+            cut = slice((at + index) * half, (at + index + 1) * half)
+            pieces += [left[:, cut], right[:, cut]]
+        return jnp.concatenate(pieces, axis=1)
+
+    g_wqkv = side_by_side(early_left, early_right, 0, 3)
+    g_wposk = side_by_side(early_left, early_right, 3, 1)
+    g_wposq = side_by_side(early_left, early_right, 4, 1)
+    g_table = side_by_side(early_left, early_right, 5, 1)[:table_rows]
+    g_wout = side_by_side(late_left, late_right, 0, 1)
+    g_wup = jnp.stack(
+        [late_left[:, half:].reshape(rows, chips, units), late_right[:, half:].reshape(rows, chips, units)], axis=2
+    ).reshape(rows, 2 * ff_half)
+    g = [vector_sum[i * rows : (i + 1) * rows] for i in range(9)]
+    g_up_bias = vector_sum[9 * rows : 9 * rows + units]
+    return (
+        hidden_out, in_grad, g_wqkv, g[0], g[1], g_table, g_wposk, g_wposq, g[2], g_wout, g[3], g[4], g[5],
+        g_wup, g_up_bias, g_wdown, g[6], g[7], g[8],
+    )
+
+
+def row_split(
     hidden_in,
     prefix,
     w_qkv,
@@ -390,7 +971,7 @@
         P(("dp", "seq"), None),
     )
     return jax.shard_map(
-        shards,
+        head_split if dict(mesh.shape) == {"dp": 16, "seq": 2} else row_split,
         mesh=mesh,
         in_specs=placed,
         out_specs=(

time: 4910 us -> 669 us (0.14)
  local copies, waits for them, and re-layouts: 2770 us -> 71.5 us
  waiting for transfers between devices: 921 us -> 138 us
  other arithmetic: 582 us -> 58.5 us
  matrix products: 413 us -> 75.5 us
  starting transfers between devices: 0.72 us -> 172 us
  Pallas kernels: 0 us -> 139 us
  blocking collectives: 126 us -> 0 us
    reshape x240 -> x5, local copies, waits for them, and re-layouts: 1090 us -> 2.66 us  [the longest x1 1.23 us: head_split(): g_wup = jnp.stack([late_left[:, half:].reshape(rows, chips, units), late_...]
    rev x72 -> x0, local copies, waits for them, and re-layouts: 670 us -> none  [skew_table(): jnp.flip(table, axis=1)]
    unnamed x23 -> x0, waiting for transfers between devices: 532 us -> none
    reduce_scatter x5 -> x0, waiting for transfers between devices: 318 us -> none  [the longest x1 142 us: shards(): lax.psum_scatter(d_wup, ('dp', 'seq'), scatter_dimension=0, tiled=True)]
    slice x193 -> x35, local copies, waits for them, and re-layouts: 248 us -> 20.5 us  [the longest x10 7.8 us: head_split(): lists[i]]
    pad x120 -> x1, local copies, waits for them, and re-layouts: 225 us -> 0.01 us  [head_split(): small = jnp.pad(small, (0, half - small.shape[0]))[None, :]]
    concatenate x48 -> x5, local copies, waits for them, and re-layouts: 217 us -> 2.28 us  [the longest x2 2 us: head_split(): jnp.concatenate([vector_own + vector_got, d_up_bias.reshape(chips, units)...]
    concatenate x48 -> x13, other arithmetic: 211 us -> 9.15 us  [the longest x4 2.6 us: side_by_side(): return jnp.concatenate(pieces, axis=1)]
  transfers between devices with their start and end apart: 18 -> 113, of which waited for: 13 -> 32; matrix products, arithmetic and copies ran while one was open for 25% -> 20% of each run, Pallas kernels for 0% -> 5%
where the time goes in v1:
time: 669 us; the launch traced here: 660 us
  starting transfers between devices  172 us (26%)
  Pallas kernels  139 us (21%)
  waiting for transfers between devices  138 us (21%)
  matrix products  75.5 us (11%)
  local copies, waits for them, and re-layouts  71.5 us (11%)
  other arithmetic  58.5 us (9%)
    pallas_call x1, Pallas kernels, attention_backward(): pl.pallas_call(backward_body, grid=(pairs, 2), in_specs=[tall, tall, tall...  104 us
    ppermute x18, starting transfers between devices, scatter_line(): up = lax.ppermute(to_above.astype(value.dtype), 'dp', ups)  66.5 us
    ppermute x12, waiting for transfers between devices, gather_pair(): other = lax.ppermute(value, 'dp', [(i, i ^ mask) for i in range(16)])  45 us
    ppermute x12, waiting for transfers between devices, scatter_pair(): other = lax.ppermute(give, 'dp', [(i, i ^ mask) for i in range(16)])  42.6 us
    dot_general x7, matrix products, product(): return jnp.dot(left, right, preferred_element_type=jnp.float32)  39.7 us
    ppermute x18, waiting for transfers between devices, gather_line(): above.append(lax.ppermute(above[-1], 'dp', down))  38.6 us
    pallas_call x1, Pallas kernels, attention_forward(): pl.pallas_call(forward_body, grid=(pairs, 2), in_specs=[pl.BlockSpec(memo...  34.9 us
    ppermute x18, starting transfers between devices, gather_line(): below.append(lax.ppermute(below[-1], 'dp', up))  34.2 us
  transfers between devices with their start and end apart: 113, of which 32 were waited for; matrix products, arithmetic and copies ran while one was open for 20% of the time, Pallas kernels for 5%

profile of v1, /device:TPU:0, one launch (start us, length us, event | category | flops | bytes accessed | tf_op | source)
XLA Modules:
  0.0 660.2 jit_solution(3624441945928111923)
XLA Ops:
  1.8 4.9 collective-permute-start.39
  41.3 7.7 %collective-permute-start.2 = (bf16[24,2304]{1,0:T(8,128)(2,1)S(1)}, bf16[24,2304]{1,0:T(8,128)(2,1)S(1)}, u32[]{:S(2)}, u32[]{:S(2)}) collective-permute-start(bf16[24,2304]{1,0:T(8,128)(2,1)S(1)} %broadcast_select_fusion.19), channel_id=1, source_target_pairs={{0,8},{2,10},{4,12},{6,14},{8,16},{10,18},{12,20},{14,22},{16,24},... | collective-permute-start | bytes 331784 | tf_op jit(solution)/shard_map/ppermute | solution.py:355
  73.2 5.5 collective-permute-done.14
  91.5 5.4 collective-permute-done.34
  102.1 7.8 %collective-permute-done.16 = bf16[4,24,2304]{2,1,0:T(8,128)(2,1)S(1)} collective-permute-done((bf16[4,24,2304]{2,1,0:T(8,128)(2,1)S(1)}, bf16[4,24,2304]{2,1,0:T(8,128)(2,1)S(1)}, u32[]{:S(2)}, u32[]{:S(2)}) %collective-permute-start.16) | collective-permute-done | bytes 442400 | tf_op jit(solution)/shard_map/ppermute | solution.py:346
  111.6 14.1 %collective-permute-done.27 = bf16[2,4,24,1920]{3,2,0,1:T(8,128)(2,1)S(1)} collective-permute-done((bf16[2,4,24,1920]{3,2,0,1:T(8,128)(2,1)S(1)}, bf16[2,4,24,1920]{3,2,0,1:T(8,128)(2,1)S(1)}, u32[]{:S(2)}, u32[]{:S(2)}) %collective-permute-start.27) | collective-permute-done | bytes 737312 | tf_op jit(solution)/shard_map/ppermute | solution.py:346
  129.5 11.9 %collective-permute-done.9 = bf16[2,4,24,2304]{3,2,1,0:T(8,128)(2,1)S(1)} collective-permute-done((bf16[2,4,24,2304]{3,2,1,0:T(8,128)(2,1)S(1)}, bf16[2,4,24,2304]{3,2,1,0:T(8,128)(2,1)S(1)}, u32[]{:S(2)}, u32[]{:S(2)}) %collective-permute-start.9) | collective-permute-done | bytes 884768 | tf_op jit(solution)/shard_map/ppermute | solution.py:346
  152.8 5.0 add_convert_fusion
  169.1 34.9 %attention_forward.1 = (bf16[1024,384]{1,0:T(8,128)(2,1)S(1)}, bf16[6,1024,1024]{2,1,0:T(8,128)(2,1)}) custom-call(s32[1]{0:T(128)S(6)} %copy.163.prefix_ref, bf16[1024,384]{1,0:T(8,128)(2,1)S(1)} %get-tuple-element.68.q_ref, bf16[1024,384]{1,0:T(8,128)(2,1)S(1)} %get-tuple-element.67.k_ref, bf16[1024,384]{1,0:T(8,128)(2,1)S(1)} %get-tuple-element.66.v_ref, ...), custom_call_target="tpu_custom_call" | custom-call | tf_op jit(solution)/shard_map/attention_forward/pallas_call | solution.py:186
  219.3 5.0 collective-permute-done.51
  236.3 5.5 collective-permute-done.53
  262.8 19.3 %multiply_convert_fusion.1 = (bf16[1024,1536]{1,0:T(8,128)(2,1)S(1)}, f32[1024,1536]{1,0:T(8,128)}, f32[1024,1536]{1,0:T(8,128)}) fusion(f32[1536]{0:T(1024)S(1)} %copy-done.88, bf16[768,1920]{1,0:T(8,128)(2,1)S(1)} %bitcast.519, bf16[512,768]{1,0:T(8,128)(2,1)S(1)} %get-tuple-element.79, bf16[512,768]{1,0:T(8,128)(2,1)S(1)} %get-tuple-element.78), kind=kOutput, calls=%fused_computation.10 | convolution fusion | flops 2522873856 | bytes 19668992 | tf_op jit(solution)/shard_map/dot_general | solution.py:35
  314.3 6.7 %fusion.129 = (bf16[1536]{0:T(1024)(128)(2,1)}, bf16[1024,1536]{1,0:T(8,128)(2,1)S(1)}) fusion(f32[1024,1536]{1,0:T(8,128)S(1)} %bitcast.548, f32[1024,1536]{1,0:T(8,128)} %get-tuple-element.221, f32[1536]{0:T(1024)S(1)} %copy-done.89, bf16[1536,384]{1,0:T(8,128)(2,1)S(1)} %bitcast.532, bf16[1536,384]{1,0:T(8,128)(2,1)S(1)} %bitcast.529, ...), kind=kOutput, calls=%fused_computation.435 | convolution fusion | flops 2441083392 | bytes 19670016 | tf_op jit(solution)/shard_map/dot_general | solution.py:45
  333.7 6.4 collective-permute-done.98
  353.4 5.2 collective-permute-start.101
  366.9 5.2 collective-permute-start.109
  388.1 104.2 %attention_backward.1 = (bf16[1024,384]{1,0:T(8,128)(2,1)S(1)}, bf16[1024,384]{1,0:T(8,128)(2,1)S(1)}, bf16[1024,384]{1,0:T(8,128)(2,1)S(1)}, f32[384,768]{1,0:T(8,128)}, f32[384,768]{1,0:T(8,128)}) custom-call(bf16[1024,384]{1,0:T(8,128)(2,1)S(1)} %get-tuple-element.68.q_ref, bf16[1024,384]{1,0:T(8,128)(2,1)S(1)} %get-tuple-element.67.k_ref, ...), custom_call_target="tpu_custom_call" | custom-call | tf_op jit(solution)/shard_map/attention_backward/pallas_call | solution.py:311
  542.8 12.3 %collective-permute-done.88 = bf16[2,4,24,1920]{3,2,1,0:T(8,128)(2,1)S(1)} collective-permute-done((bf16[2,4,24,1920]{3,2,1,0:T(8,128)(2,1)S(1)}, bf16[2,4,24,1920]{3,2,1,0:T(8,128)(2,1)S(1)}, u32[]{:S(2)}, u32[]{:S(2)}) %collective-permute-start.88) | collective-permute-done | bytes 737312 | tf_op jit(solution)/shard_map/ppermute | solution.py:367
  557.9 16.2 %collective-permute-done.70 = bf16[2,4,24,2304]{3,2,1,0:T(8,128)(2,1)S(1)} collective-permute-done((bf16[2,4,24,2304]{3,2,1,0:T(8,128)(2,1)S(1)}, bf16[2,4,24,2304]{3,2,1,0:T(8,128)(2,1)S(1)}, u32[]{:S(2)}, u32[]{:S(2)}) %collective-permute-start.70) | collective-permute-done | bytes 884768 | tf_op jit(solution)/shard_map/ppermute | solution.py:367
  575.9 6.9 %collective-permute-done.89 = bf16[4,24,1920]{2,1,0:T(8,128)(2,1)S(1)} collective-permute-done((bf16[4,24,1920]{2,1,0:T(8,128)(2,1)S(1)}, bf16[4,24,1920]{2,1,0:T(8,128)(2,1)S(1)}, u32[]{:S(2)}, u32[]{:S(2)}) %collective-permute-start.89) | collective-permute-done | bytes 368672 | tf_op jit(solution)/shard_map/ppermute | solution.py:367
  598.5 5.2 collective-permute-start.92
  605.1 5.2 collective-permute-start.84
  635.8 4.8 collective-permute-start.74
  642.0 5.2 collective-permute-start.66
  (696 shorter events, 345.0 us)
Async XLA Ops:
  1.8 33.9 %collective-permute-start.39 = (bf16[96,384]{1,0:T(8,128)(2,1)S(1)}, bf16[96,384]{1,0:T(8,128)(2,1)S(1)}, u32[]{:S(2)}, u32[]{:S(2)}) collective-permute-start(bf16[96,384]{1,0:T(8,128)(2,1)S(1)} %slice.625), channel_id=1, source_target_pairs={{0,8},{2,10},{4,12},{6,14},{8,16},{10,18},{12,20},{14,22},{16,24},... | collective-permute-start | bytes 221192 | tf_op jit(solution)/shard_map/ppermute | solution.py:355
  35.7 22.0 %collective-permute-start.42 = (bf16[96,384]{1,0:T(8,128)(2,1)S(1)}, bf16[96,384]{1,0:T(8,128)(2,1)S(1)}, u32[]{:S(2)}, u32[]{:S(2)}) collective-permute-start(bf16[96,384]{1,0:T(8,128)(2,1)S(1)} %slice.625), channel_id=1, source_target_pairs={{8,0},{10,2},{12,4},{14,6},{16,8},{18,10},{20,12},{22,14},{24,16},... | collective-permute-start | bytes 221192 | tf_op jit(solution)/shard_map/ppermute | solution.py:356
  37.1 24.0 %collective-permute-start.40 = (bf16[96,384]{1,0:T(8,128)(2,1)S(1)}, bf16[96,384]{1,0:T(8,128)(2,1)}, u32[]{:S(2)}, u32[]{:S(2)}) collective-permute-start(bf16[96,384]{1,0:T(8,128)(2,1)S(1)} %collective-permute-done.39), channel_id=1, source_target_pairs={{8,16},{10,18},{12,20},{14,22},{16,24},{18,26},{20,28},{22,30},{9,... | collective-permute-start | bytes 221192 | tf_op jit(solution)/shard_map/ppermute | solution.py:355
  71.9 26.7 %collective-permute-start = (bf16[512,768]{1,0:T(8,128)(2,1)S(1)}, bf16[512,768]{1,0:T(8,128)(2,1)S(1)}, u32[]{:S(2)}, u32[]{:S(2)}) collective-permute-start(bf16[512,768]{1,0:T(8,128)(2,1)S(1)} %copy-done.18), channel_id=1, source_target_pairs={{0,1},{1,0},{2,3},{3,2},{4,5},{5,4},{6,7},{7,6},{8,9},{9,8},{10,11... | collective-permute-start | bytes 2359304 | tf_op jit(solution)/shard_map/ppermute | solution.py:331
  71.9 135.2 %collective-permute-start.41 = (bf16[96,384]{1,0:T(8,128)(2,1)}, bf16[96,384]{1,0:T(8,128)(2,1)}, u32[]{:S(2)}, u32[]{:S(2)}) collective-permute-start(bf16[96,384]{1,0:T(8,128)(2,1)} %collective-permute-done.40), channel_id=1, source_target_pairs={{16,24},{18,26},{20,28},{22,30},{17,25},{19,27},{21,29},{23,31}} | collective-permute-start | bytes 221192 | tf_op jit(solution)/shard_map/ppermute | solution.py:355
  78.6 128.4 %collective-permute-start.44 = (bf16[96,384]{1,0:T(8,128)(2,1)}, bf16[96,384]{1,0:T(8,128)(2,1)}, u32[]{:S(2)}, u32[]{:S(2)}) collective-permute-start(bf16[96,384]{1,0:T(8,128)(2,1)} %collective-permute-done.43), channel_id=1, source_target_pairs={{8,0},{10,2},{12,4},{14,6},{9,1},{11,3},{13,5},{15,7}} | collective-permute-start | bytes 221192 | tf_op jit(solution)/shard_map/ppermute | solution.py:356
  98.6 27.1 %collective-permute-start.27 = (bf16[2,4,24,1920]{3,2,0,1:T(8,128)(2,1)S(1)}, bf16[2,4,24,1920]{3,2,0,1:T(8,128)(2,1)S(1)}, u32[]{:S(2)}, u32[]{:S(2)}) collective-permute-start(bf16[2,4,24,1920]{3,2,0,1:T(8,128)(2,1)S(1)} %pad_maximum_fusion.21), channel_id=1, source_target_pairs={{0,4},{2,6},{4,0},{6,2},{8,12},{10,14},{12,8},{14,10},{16,20},{18,... | collective-permute-start | bytes 2211848 | tf_op jit(solution)/shard_map/ppermute | solution.py:346
  100.5 26.9 %collective-permute-start.35 = (bf16[2,4,24,1920]{3,2,1,0:T(8,128)(2,1)S(1)}, bf16[2,4,24,1920]{3,2,1,0:T(8,128)(2,1)S(1)}, u32[]{:S(2)}, u32[]{:S(2)}) collective-permute-start(bf16[2,4,24,1920]{3,2,1,0:T(8,128)(2,1)S(1)} %pad_maximum_fusion.22), channel_id=1, source_target_pairs={{0,2},{2,0},{4,6},{6,4},{8,10},{10,8},{12,14},{14,12},{16,18},{18,... | collective-permute-start | bytes 2211848 | tf_op jit(solution)/shard_map/ppermute | solution.py:346
  109.9 31.5 %collective-permute-start.9 = (bf16[2,4,24,2304]{3,2,1,0:T(8,128)(2,1)S(1)}, bf16[2,4,24,2304]{3,2,1,0:T(8,128)(2,1)S(1)}, u32[]{:S(2)}, u32[]{:S(2)}) collective-permute-start(bf16[2,4,24,2304]{3,2,1,0:T(8,128)(2,1)S(1)} %pad_maximum_fusion.18), channel_id=1, source_target_pairs={{0,4},{2,6},{4,0},{6,2},{8,12},{10,14},{12,8},{14,10},{16,20},{18,... | collective-permute-start | bytes 2654216 | tf_op jit(solution)/shard_map/ppermute | solution.py:346
  129.5 28.3 %collective-permute-start.36 = (bf16[384,384]{1,0:T(8,128)(2,1)}, bf16[384,384]{1,0:T(8,128)(2,1)}, u32[]{:S(2)}, u32[]{:S(2)}) collective-permute-start(bf16[384,384]{1,0:T(8,128)(2,1)} %constant_dynamic-slice_fusion.2), channel_id=1, source_target_pairs={{0,1},{1,0},{2,3},{3,2},{4,5},{5,4},{6,7},{7,6},{8,9},{9,8},{10,11... | collective-permute-start | bytes 884744 | tf_op jit(solution)/shard_map/ppermute | solution.py:331
  206.7 41.5 %collective-permute-start.37 = (f32[512,768]{1,0:T(8,128)}, f32[512,768]{1,0:T(8,128)}, u32[]{:S(2)}, u32[]{:S(2)}) collective-permute-start(f32[512,768]{1,0:T(8,128)} %fusion.74), channel_id=1, source_target_pairs={{0,1},{1,0},{2,3},{3,2},{4,5},{5,4},{6,7},{7,6},{8,9},{9,8},{10,11... | collective-permute-start | bytes 4718600 | tf_op jit(solution)/shard_map/ppermute | solution.py:331
  309.6 19.2 %collective-permute-start.97 = (bf16[2,4,96,384]{3,2,1,0:T(8,128)(2,1)}, bf16[2,4,96,384]{3,2,1,0:T(8,128)(2,1)}, u32[]{:S(2)}, u32[]{:S(2)}) collective-permute-start(bf16[2,4,96,384]{3,2,1,0:T(8,128)(2,1)} %select_bitcast_fusion.13), channel_id=1, source_target_pairs={{0,2},{2,0},{4,6},{6,4},{8,10},{10,8},{12,14},{14,12},{16,18},{18,... | collective-permute-start | bytes 1769480 | tf_op jit(solution)/shard_map/ppermute | solution.py:367
  327.4 32.5 %collective-permute-start.57 = (f32[512,768]{1,0:T(8,128)}, f32[512,768]{1,0:T(8,128)}, u32[]{:S(2)}, u32[]{:S(2)}) collective-permute-start(f32[512,768]{1,0:T(8,128)} %fusion.16), channel_id=1, source_target_pairs={{0,1},{1,0},{2,3},{3,2},{4,5},{5,4},{6,7},{7,6},{8,9},{9,8},{10,11... | collective-permute-start | bytes 4718600 | tf_op jit(solution)/shard_map/ppermute | solution.py:331
  353.4 19.9 %collective-permute-start.101 = (bf16[96,384]{1,0:T(8,128)(2,1)S(1)}, bf16[96,384]{1,0:T(8,128)(2,1)S(1)}, u32[]{:S(2)}, u32[]{:S(2)}) collective-permute-start(bf16[96,384]{1,0:T(8,128)(2,1)S(1)} %get-tuple-element.144), channel_id=1, source_target_pairs={{0,8},{2,10},{4,12},{6,14},{8,16},{10,18},{12,20},{14,22},{16,24},... | collective-permute-start | bytes 221192 | tf_op jit(solution)/shard_map/ppermute | solution.py:384
  509.2 23.1 %collective-permute-start.79 = (bf16[384,384]{1,0:T(8,128)(2,1)}, bf16[384,384]{1,0:T(8,128)(2,1)}, u32[]{:S(2)}, u32[]{:S(2)}) collective-permute-start(bf16[384,384]{1,0:T(8,128)(2,1)} %constant_dynamic-slice_fusion), channel_id=1, source_target_pairs={{0,1},{1,0},{2,3},{3,2},{4,5},{5,4},{6,7},{7,6},{8,9},{9,8},{10,11... | collective-permute-start | bytes 884744 | tf_op jit(solution)/shard_map/ppermute | solution.py:331
  530.2 80.1 %collective-permute-start.59 = (f32[512,768]{1,0:T(8,128)}, f32[512,768]{1,0:T(8,128)S(1)}, u32[]{:S(2)}, u32[]{:S(2)}) collective-permute-start(f32[512,768]{1,0:T(8,128)} %fusion.40), channel_id=1, source_target_pairs={{0,1},{1,0},{2,3},{3,2},{4,5},{5,4},{6,7},{7,6},{8,9},{9,8},{10,11... | collective-permute-start | bytes 4718600 | tf_op jit(solution)/shard_map/ppermute | solution.py:331
  535.7 19.4 %collective-permute-start.88 = (bf16[2,4,24,1920]{3,2,1,0:T(8,128)(2,1)S(1)}, bf16[2,4,24,1920]{3,2,1,0:T(8,128)(2,1)S(1)}, u32[]{:S(2)}, u32[]{:S(2)}) collective-permute-start(bf16[2,4,24,1920]{3,2,1,0:T(8,128)(2,1)S(1)} %select_bitcast_fusion.6), channel_id=1, source_target_pairs={{0,4},{2,6},{4,0},{6,2},{8,12},{10,14},{12,8},{14,10},{16,20},{18,... | collective-permute-start | bytes 2211848 | tf_op jit(solution)/shard_map/ppermute | solution.py:367
  536.5 19.9 %collective-permute-start.80 = (bf16[2,4,24,1920]{3,2,1,0:T(8,128)(2,1)S(1)}, bf16[2,4,24,1920]{3,2,1,0:T(8,128)(2,1)S(1)}, u32[]{:S(2)}, u32[]{:S(2)}) collective-permute-start(bf16[2,4,24,1920]{3,2,1,0:T(8,128)(2,1)S(1)} %select_bitcast_fusion.7), channel_id=1, source_target_pairs={{0,2},{2,0},{4,6},{6,4},{8,10},{10,8},{12,14},{14,12},{16,18},{18,... | collective-permute-start | bytes 2211848 | tf_op jit(solution)/shard_map/ppermute | solution.py:367
  539.8 34.3 %collective-permute-start.70 = (bf16[2,4,24,2304]{3,2,1,0:T(8,128)(2,1)S(1)}, bf16[2,4,24,2304]{3,2,1,0:T(8,128)(2,1)S(1)}, u32[]{:S(2)}, u32[]{:S(2)}) collective-permute-start(bf16[2,4,24,2304]{3,2,1,0:T(8,128)(2,1)S(1)} %select_bitcast_fusion), channel_id=1, source_target_pairs={{0,4},{2,6},{4,0},{6,2},{8,12},{10,14},{12,8},{14,10},{16,20},{18,... | collective-permute-start | bytes 2654216 | tf_op jit(solution)/shard_map/ppermute | solution.py:367
  541.7 33.8 %collective-permute-start.62 = (bf16[2,4,24,2304]{3,2,1,0:T(8,128)(2,1)S(1)}, bf16[2,4,24,2304]{3,2,1,0:T(8,128)(2,1)S(1)}, u32[]{:S(2)}, u32[]{:S(2)}) collective-permute-start(bf16[2,4,24,2304]{3,2,1,0:T(8,128)(2,1)S(1)} %select_bitcast_fusion.1), channel_id=1, source_target_pairs={{0,2},{2,0},{4,6},{6,4},{8,10},{10,8},{12,14},{14,12},{16,18},{18,... | collective-permute-start | bytes 2654216 | tf_op jit(solution)/shard_map/ppermute | solution.py:367
  555.5 27.3 %collective-permute-start.89 = (bf16[4,24,1920]{2,1,0:T(8,128)(2,1)S(1)}, bf16[4,24,1920]{2,1,0:T(8,128)(2,1)S(1)}, u32[]{:S(2)}, u32[]{:S(2)}) collective-permute-start(bf16[4,24,1920]{2,1,0:T(8,128)(2,1)S(1)} %select_bitcast_fusion.24), channel_id=1, source_target_pairs={{0,2},{2,0},{4,6},{6,4},{8,10},{10,8},{12,14},{14,12},{16,18},{18,... | collective-permute-start | bytes 1105928 | tf_op jit(solution)/shard_map/ppermute | solution.py:367
  556.8 30.5 %collective-permute-start.81 = (bf16[4,24,1920]{2,1,0:T(8,128)(2,1)S(1)}, bf16[4,24,1920]{2,1,0:T(8,128)(2,1)S(1)}, u32[]{:S(2)}, u32[]{:S(2)}) collective-permute-start(bf16[4,24,1920]{2,1,0:T(8,128)(2,1)S(1)} %select_bitcast_fusion.25), channel_id=1, source_target_pairs={{0,4},{2,6},{4,0},{6,2},{8,12},{10,14},{12,8},{14,10},{16,20},{18,... | collective-permute-start | bytes 1105928 | tf_op jit(solution)/shard_map/ppermute | solution.py:367
  574.5 42.5 %collective-permute-start.71 = (bf16[4,24,2304]{2,1,0:T(8,128)(2,1)S(1)}, bf16[4,24,2304]{2,1,0:T(8,128)(2,1)S(1)}, u32[]{:S(2)}, u32[]{:S(2)}) collective-permute-start(bf16[4,24,2304]{2,1,0:T(8,128)(2,1)S(1)} %select_bitcast_fusion.18), channel_id=1, source_target_pairs={{0,2},{2,0},{4,6},{6,4},{8,10},{10,8},{12,14},{14,12},{16,18},{18,... | collective-permute-start | bytes 1327112 | tf_op jit(solution)/shard_map/ppermute | solution.py:367
  616.9 31.6 %collective-permute-start.96 = (f32[24,1920]{1,0:T(8,128)S(1)}, f32[24,1920]{1,0:T(8,128)S(1)}, u32[]{:S(2)}, u32[]{:S(2)}) collective-permute-start(f32[24,1920]{1,0:T(8,128)S(1)} %get-tuple-element.45), channel_id=1, source_target_pairs={{0,1},{1,0},{2,3},{3,2},{4,5},{5,4},{6,7},{7,6},{8,9},{9,8},{10,11... | collective-permute-start | bytes 552968 | tf_op jit(solution)/shard_map/ppermute | solution.py:331
  (198 other events, 1940.6 us)
